TPU v7x, 512 devices: a whole 4x8x8 slice. The times are simulated.
512 devices in a mesh: dp: 64 (over y, x, core), tensor: 8 (over z).
Axes of the slice: x: 4, y: 8, z: 8, core: 2. Of those that a mesh axis runs over, the one named last changes fastest.
Arguments:
- hidden_act: bfloat16 [32768, 1408], P('dp', 'tensor'), may hold values from -6 to 6
- cotangent: bfloat16 [32768, 2048], P('dp', 'tensor'), may hold values from -4 to 4
- down_table: bfloat16 [1408, 64, 2048], P('tensor', 'dp'), may hold values from -0.15625 to 0.15625
- expert_ids: int32 [128, 4], P('dp'), may hold values from 0 to 31, as said below
- merge_weights: float32 [128, 4], P('dp'), may hold values from 0.1 to 1
- owner_slot: int32 [32], replicated, may hold values from 0 to 63, as said below
Outputs:
- layer_out: bfloat16 [32768, 2048], P('dp', 'tensor')
- grad_hidden: bfloat16 [32768, 1408], P('dp', 'tensor')
- expert_grad: float32 [1408, 64, 2048], P('tensor', 'dp')
Inputs may be any that keep to these rules, and one draw needn't show every extreme that they name: `expert_ids`: each segment lists 4 different experts; the 2 segments of one index of dp list exactly 6 different experts together. `owner_slot`: different experts have different slots; slot 63 always holds an expert.
All inputs are finite; a program needn't handle non-finite values.
Results may differ from a plain program's by a relative error of at most 0.013.
Values may be sent and summed in bfloat16 or wider, within the bound.
A program may use at most 128 MiB of HBM per device.

v0:
```python
import jax
import jax.numpy as jnp
from jax import lax
from jax.sharding import PartitionSpec as P

E = 32
K = 4
POOL = 6


def pool_members(id_rows):
    listed = id_rows.reshape(-1)
    experts = jnp.arange(E, dtype=jnp.int32)
    present = jnp.any(listed[None, :] == experts[:, None], axis=1)
    ranking = jnp.cumsum(present.astype(jnp.int32)) - 1
    places = jnp.arange(POOL, dtype=jnp.int32)
    chosen = present[None, :] & (ranking[None, :] == places[:, None])
    return jnp.sum(jnp.where(chosen, experts[None, :], 0), axis=1)


def merge_coefficients(id_rows, weight_rows, targets):
    matches = id_rows[:, :, None] == targets[None, None, :]
    return jnp.sum(jnp.where(matches, weight_rows[:, :, None], 0.0), axis=1)


def body(hidden_act, cotangent, down_table, expert_ids, merge_weights, owner_slot):
    dp_count = lax.axis_size("dp")
    seg_count = expert_ids.shape[0]
    ff_local, slot_local, width = down_table.shape
    stripe = width // dp_count
    row_count = hidden_act.shape[0]
    seg_len = row_count // seg_count
    every_expert = jnp.arange(E, dtype=jnp.int32)
    all_ids, all_weights = (
        lax.all_gather(expert_ids, "dp", axis=0, tiled=True),
        lax.all_gather(merge_weights, "dp", axis=0, tiled=True),
    )
    ids_by_dev = all_ids.reshape(dp_count, seg_count, K)
    weights_by_dev = all_weights.reshape(dp_count, seg_count, K)
    pools_all = jax.vmap(pool_members)(ids_by_dev)
    my_pool = pools_all[lax.axis_index("dp")]
    my_coef = merge_coefficients(expert_ids, merge_weights, my_pool)
    member_table = (pools_all.T[:, :, None] == every_expert[None, None, :]).astype(jnp.bfloat16)
    stripes = lax.all_to_all(down_table, "dp", split_axis=2, concat_axis=1, tiled=True)
    by_expert = jnp.take(stripes, owner_slot, axis=1)
    outgoing = jnp.take(by_expert, pools_all.T, axis=1).reshape(ff_local, POOL, width)
    panel_set = lax.all_to_all(outgoing, "dp", split_axis=2, concat_axis=2, tiled=True)
    merged = jnp.sum(
        panel_set[:, None, :, :].astype(jnp.float32) * my_coef[None, :, :, None], axis=2
    ).astype(jnp.bfloat16)
    hidden_seg = hidden_act.reshape(seg_count, seg_len, ff_local)
    partial_rows = jnp.einsum(
        "stf,fsd->std", hidden_seg, merged, preferred_element_type=jnp.float32
    ).reshape(row_count, width)
    layer_out = lax.psum_scatter(
        partial_rows.astype(jnp.bfloat16), "tensor", scatter_dimension=1, tiled=True
    )
    full_cot = lax.all_gather(cotangent, "tensor", axis=1, tiled=True)
    cot_seg = full_cot.reshape(seg_count, seg_len, width)
    grad_hidden = (
        jnp.einsum("std,fsd->stf", cot_seg, merged, preferred_element_type=jnp.float32)
        .astype(jnp.bfloat16)
        .reshape(row_count, ff_local)
    )
    seg_grads = jnp.einsum(
        "stf,std->fsd", hidden_seg, cot_seg, preferred_element_type=jnp.float32
    ).astype(jnp.bfloat16)
    returned = lax.all_to_all(seg_grads, "dp", split_axis=2, concat_axis=2, tiled=True).reshape(
        ff_local, seg_count, dp_count, stripe
    )
    pool_coef = jax.vmap(merge_coefficients)(ids_by_dev, weights_by_dev, pools_all)
    coef_view = jnp.transpose(pool_coef, (1, 2, 0))
    group_sums = jnp.sum(
        returned[:, :, None, :, :].astype(jnp.float32) * coef_view[None, :, :, :, None], axis=1
    ).astype(jnp.bfloat16)
    grad_stripes = jnp.einsum(
        "fprd,pre->fed", group_sums, member_table, preferred_element_type=jnp.float32
    )
    slotted = (
        jnp.zeros((ff_local, slot_local * dp_count, stripe), jnp.float32)
        .at[:, owner_slot, :]
        .set(grad_stripes)
    )
    expert_grad = lax.all_to_all(
        slotted.astype(jnp.bfloat16), "dp", split_axis=1, concat_axis=2, tiled=True
    ).astype(slotted.dtype)
    return (layer_out, grad_hidden, expert_grad)


def solution(mesh):
    placed = (
        P("dp", "tensor"),
        P("dp", "tensor"),
        P("tensor", "dp", None),
        P("dp", None),
        P("dp", None),
        P(),
    )
    return jax.shard_map(
        body,
        mesh=mesh,
        in_specs=placed,
        out_specs=(P("dp", "tensor"), P("dp", "tensor"), P("tensor", "dp", None)),
        check_vma=False,
    )
```

profile of v0, /device:TPU:1, one launch (start us, length us, event | category | flops | bytes accessed | tf_op | source)
XLA Modules:
  0.0 478.6 jit_solution(9711148216334973201)
XLA Ops:
  7.2 4.5 copy.81
  12.2 11.6 %reduce.2 = bf16[2048,176]{1,0:T(8,128)(2,1)S(1)} reduce(bf16[2048,1,176]{2,1,0:T(2,128)(2,1)S(1)} %bitcast.55, bf16[]{:T(256)} %broadcast.42), dimensions={1}, to_apply=%bitcast.44.reduce_sub_computation | reduce | bytes 1441794
  23.9 2.6 reshape.124
  26.5 11.6 %all-to-all-start = ((bf16[64,2,2816]{2,1,0:T(2,128)(2,1)}), bf16[64,2,2816]{2,1,0:T(2,128)(2,1)S(1)}, u32[]{:S(2)}, u32[]{:S(2)}) async-start(bf16[64,2,2816]{2,1,0:T(2,128)(2,1)} %reshape.124), calls=%async_computation | async-start | bytes 1441792 | tf_op jit(solution)/shard_map/all_to_all | solution.py:44
  38.1 50.6 %all-gather = s32[64,2,4]{2,1,0:T(2,128)S(1)} all-gather(s32[1,2,4]{2,1,0:T(2,128)S(1)} %bitcast.65), channel_id=1, replica_groups=mesh['dp'=64,'tensor'=8] {'dp'}, dimensions={0}, use_global_device_ids=true | all-gather | bytes 2080 | tf_op jit(solution)/shard_map/all_gather | solution.py:35
  89.8 3.2 reshape.125
  93.8 13.3 %gather_fusion.1 = bf16[384,176,32]{1,2,0:T(8,128)(2,1)} fusion(bf16[176,32,32]{0,2,1:T(8,128)(2,1)S(1)} %select_bitcast_fusion, s32[1024]{0:T(1024)S(1)} %pad_clamp_fusion), kind=kCustom, calls=%fused_computation.1 | custom fusion | bytes 8652288 | tf_op jit(solution)/shard_map/jit(_take)/gather | solution.py:46
  107.2 6.2 %broadcast_select_fusion = bf16[176,6,2048]{0,2,1:T(8,128)(2,1)S(1)} fusion(bf16[176,6,2048]{0,2,1:T(8,128)(2,1)} %bitcast.51, pred[6,2048]{1,0:T(8,128)(4,1)S(1)} %broadcast_in_dim.86), kind=kLoop, calls=%fused_computation.7 | loop fusion | flops 2162688 | bytes 8663040 | tf_op jit(solution)/shard_map/jit(_take)/select_n | solution.py:46
  113.4 22.3 %copy.82 = bf16[176,6,2048]{0,1,2:T(8,128)(2,1)} copy(bf16[176,6,2048]{0,2,1:T(8,128)(2,1)S(1)} %broadcast_select_fusion) | data formatting | bytes 8650752 | tf_op jit(solution)/shard_map/jit(_take)/select_n | solution.py:46
  135.7 8.6 %all-to-all-start.1 = ((bf16[176,6,2048]{0,1,2:T(8,128)(2,1)}), bf16[176,6,2048]{0,1,2:T(8,128)(2,1)}, u32[]{:S(2)}, u32[]{:S(2)}) async-start(bf16[176,6,2048]{0,1,2:T(8,128)(2,1)} %copy.82), calls=%async_computation.1 | async-start | bytes 16777216 | tf_op jit(solution)/shard_map/all_to_all | solution.py:47
  145.1 53.0 %all-gather.4.cloned.1.call-done = bf16[512,2048]{1,0:T(8,128)(2,1)} async-done(((bf16[512,256]{1,0:T(8,128)(2,1)}), bf16[512,2048]{1,0:T(8,128)(2,1)}) %all-gather.4.cloned.1.call-update) | async-done | bytes 2097168 | tf_op jit(solution)/shard_map/all_gather | solution.py:58
  198.0 2.1 fusion.2
  200.2 3.8 copy.87
  204.0 122.7 %all-to-all-done.1 = bf16[176,6,2048]{0,1,2:T(8,128)(2,1)} async-done(((bf16[176,6,2048]{0,1,2:T(8,128)(2,1)}), bf16[176,6,2048]{0,1,2:T(8,128)(2,1)}, u32[]{:S(2)}, u32[]{:S(2)}) %all-to-all-start.1) | async-done | bytes 4325408 | tf_op jit(solution)/shard_map/all_to_all | solution.py:47
  326.7 10.1 %all-to-all-start.2 = ((bf16[176,2,2048]{0,1,2:T(2,128)(2,1)}), bf16[176,2,2048]{0,1,2:T(2,128)(2,1)S(1)}, u32[]{:S(2)}, u32[]{:S(2)}) async-start(bf16[176,2,2048]{0,1,2:T(2,128)(2,1)} %copy.87), calls=%async_computation.3 | async-start | bytes 4194304 | tf_op jit(solution)/shard_map/all_to_all | solution.py:68
  337.1 11.3 %copy.83 = bf16[176,6,2048]{2,0,1:T(8,128)(2,1)} copy(bf16[176,6,2048]{0,1,2:T(8,128)(2,1)} %all-to-all-done.1) | data formatting | bytes 8650752 | tf_op jit(solution)/shard_map/all_to_all | solution.py:47
  348.4 6.6 %convert_element_type.68 = f32[176,6,2048]{2,0,1:T(8,128)} convert(bf16[176,6,2048]{2,0,1:T(8,128)(2,1)} %copy.83) | non-fusion elementwise | flops 2162688 | bytes 12976128 | tf_op jit(solution)/shard_map/convert_element_type | solution.py:49
  355.0 4.8 multiply_reduce_fusion.1
  360.9 2.1 convolution_convert_fusion
  363.0 53.9 %all-gather.1 = f32[64,2,4]{2,1,0:T(2,128)S(1)} all-gather(f32[1,2,4]{2,1,0:T(2,128)S(1)} %bitcast.66), channel_id=1, replica_groups=mesh['dp'=64,'tensor'=8] {'dp'}, dimensions={0}, use_global_device_ids=true | all-gather | bytes 2080 | tf_op jit(solution)/shard_map/all_gather | solution.py:36
  417.7 4.2 multiply_reduce_fusion
  421.9 3.7 fusion.3
  428.2 35.5 %all_to_all.31 = bf16[176,64,32]{0,2,1:T(8,128)(2,1)S(1)} all-to-all(bf16[176,64,32]{0,2,1:T(8,128)(2,1)S(1)} %convert_element_type.80), channel_id=1, replica_groups=mesh['dp'=64,'tensor'=8] {'dp'}, dimensions={1} | all-to-all | bytes 1441792 | tf_op jit(solution)/shard_map/all_to_all | solution.py:84
  465.2 5.1 %copy.93 = f32[176,1,2048]{2,1,0:T(1,128)} copy(f32[176,1,2048]{0,2,1:T(8,128)} %bitcast_convert_fusion) | data formatting | bytes 2883584
  (54 shorter events, 10.8 us)
Async XLA Ops:
  23.9 14.3 %copy-start.4 = (s32[2,4]{1,0:T(2,128)S(1)}, s32[2,4]{1,0:T(2,128)}, u32[]{:S(2)}) copy-start(s32[2,4]{1,0:T(2,128)} %param.9) | copy-start | bytes 100
  23.9 65.9 %copy-start.6 = (s32[32]{0:T(128)S(1)}, s32[32]{0:T(128)}, u32[]{:S(2)}) copy-start(s32[32]{0:T(128)} %param.11) | copy-start | bytes 388
  26.5 63.3 %all-to-all-start = ((bf16[64,2,2816]{2,1,0:T(2,128)(2,1)}), bf16[64,2,2816]{2,1,0:T(2,128)(2,1)S(1)}, u32[]{:S(2)}, u32[]{:S(2)}) async-start(bf16[64,2,2816]{2,1,0:T(2,128)(2,1)} %reshape.124), calls=%async_computation | async-start | bytes 1441792 | tf_op jit(solution)/shard_map/all_to_all | solution.py:44
  135.7 62.3 %copy-start.3 = (bf16[512,176]{0,1:T(8,128)(2,1)S(1)}, bf16[512,176]{0,1:T(8,128)(2,1)}, u32[]{:S(2)}) copy-start(bf16[512,176]{0,1:T(8,128)(2,1)} %param.6) | copy-start | bytes 540676
  135.7 191.0 %all-to-all-start.1 = ((bf16[176,6,2048]{0,1,2:T(8,128)(2,1)}), bf16[176,6,2048]{0,1,2:T(8,128)(2,1)}, u32[]{:S(2)}, u32[]{:S(2)}) async-start(bf16[176,6,2048]{0,1,2:T(8,128)(2,1)} %copy.82), calls=%async_computation.1 | async-start | bytes 16777216 | tf_op jit(solution)/shard_map/all_to_all | solution.py:47
  144.3 53.7 %all-gather.4.cloned.1.call-start = ((), (), s32[]{:S(2)}) async-start(), calls=%async_computation.6 | async-start | bytes 2359296 | tf_op jit(solution)/shard_map/all_gather | solution.py:58
  204.0 133.0 %copy-start.5 = (f32[2,4]{1,0:T(2,128)S(1)}, f32[2,4]{1,0:T(2,128)}, u32[]{:S(2)}) copy-start(f32[2,4]{1,0:T(2,128)} %param.10) | copy-start | bytes 100
  326.7 90.3 %all-to-all-start.2 = ((bf16[176,2,2048]{0,1,2:T(2,128)(2,1)}), bf16[176,2,2048]{0,1,2:T(2,128)(2,1)S(1)}, u32[]{:S(2)}, u32[]{:S(2)}) async-start(bf16[176,2,2048]{0,1,2:T(2,128)(2,1)} %copy.87), calls=%async_computation.3 | async-start | bytes 4194304 | tf_op jit(solution)/shard_map/all_to_all | solution.py:68
  336.8 135.0 %reduce-scatter.2.cloned.1.call-start = ((), (), s32[]{:S(2)}) async-start(), calls=%async_computation.5 | async-start | bytes 2359296 | tf_op jit(solution)/shard_map/reduce_scatter | solution.py:55
  359.8 1.1 copy-start
  465.2 5.1 %copy-start.1 = (bf16[176,2,2048]{2,0,1:T(8,128)(2,1)S(1)}, bf16[176,2,2048]{2,0,1:T(8,128)(2,1)}, u32[]{:S(2)}) copy-start(bf16[176,2,2048]{2,0,1:T(8,128)(2,1)} %copy-done) | copy-start | bytes 4325380
  465.2 5.1 %copy-start.2 = (bf16[512,2048]{1,0:T(8,128)(2,1)S(1)}, bf16[512,2048]{1,0:T(8,128)(2,1)}, u32[]{:S(2)}) copy-start(bf16[512,2048]{1,0:T(8,128)(2,1)} %all-gather.4.cloned.1.call-done) | copy-start | bytes 6291460
Sparse Core Ops, SparseCore 0:
  147.2 50.8 all-gather.3
  363.1 45.3 reduce-scatter.1
where the time goes:
time: 480 us; the launch traced here: 479 us
  waiting for transfers between devices  176 us (37%)
  blocking collectives  140 us (29%)
  local copies, waits for them, and re-layouts  72.6 us (15%)
  other arithmetic  36.2 us (8%)
  starting transfers between devices  30.4 us (6%)
  between operations  14.3 us (3%)
  matrix products  8.77 us (2%)
    all_to_all x1, waiting for transfers between devices, body(): lax.all_to_all(outgoing, 'dp', split_axis=2, concat_axis=2, tiled=True)  123 us
    all_gather x1, blocking collectives, body(): lax.all_gather(merge_weights, 'dp', axis=0, tiled=True)  53.9 us
    all_gather x1, waiting for transfers between devices, body(): full_cot = lax.all_gather(cotangent, 'tensor', axis=1, tiled=True)  53 us
    all_gather x1, blocking collectives, body(): lax.all_gather(expert_ids, 'dp', axis=0, tiled=True)  50.6 us
    all_to_all x1, blocking collectives, body(): lax.all_to_all(slotted.astype(jnp.bfloat16), 'dp', split_axis=1, concat_a...  35.5 us
    select_n x1, local copies, waits for them, and re-layouts, body(): jnp.take(by_expert, pools_all.T, axis=1).reshape(ff_local, POOL, width)  22.3 us
    unnamed x20, local copies, waits for them, and re-layouts  17.2 us
    gather x1, local copies, waits for them, and re-layouts, body(): jnp.take(by_expert, pools_all.T, axis=1).reshape(ff_local, POOL, width)  13.3 us
  transfers between devices with their start and end apart: 5, of which 2 were waited for; matrix products, arithmetic and copies ran while one was open for 11% of the time, Pallas kernels for 0%

commit v1 on v0

v1 whole, which is shorter than its diff:
```python
import jax
import jax.numpy as jnp
from jax import lax
from jax.sharding import PartitionSpec as P

E = 32
K = 4
ROW_PARTS = 4
PAD = 4


def two_pieces(values):
    high = lax.reduce_precision(values, 8, 7)
    low = lax.reduce_precision(values - high, 8, 7)
    return high, low


def exchange(blocks):
    return lax.all_to_all(blocks, "dp", split_axis=0, concat_axis=0, tiled=True)


def split_panels(panels, count):
    lead, ff_local, width = panels.shape
    cols = count // ROW_PARTS
    view = panels.reshape(lead, ROW_PARTS, ff_local // ROW_PARTS, cols, width // cols)
    return jnp.transpose(view, (1, 3, 0, 2, 4)).reshape(
        count, lead, ff_local // ROW_PARTS, width // cols
    )


def join_panels(chunks):
    count, lead, rows, lanes = chunks.shape
    cols = count // ROW_PARTS
    view = chunks.reshape(ROW_PARTS, cols, lead, rows, lanes)
    return jnp.transpose(view, (2, 0, 3, 1, 4)).reshape(lead, ROW_PARTS * rows, cols * lanes)


def body(hidden_act, cotangent, down_table, expert_ids, merge_weights, owner_slot):
    count = lax.axis_size("dp")
    seg_count = expert_ids.shape[0]
    ff_local, _, width = down_table.shape
    row_count = hidden_act.shape[0]
    seg_len = row_count // seg_count
    rows = ff_local // ROW_PARTS
    lanes = width * ROW_PARTS // count
    listed = seg_count * K

    full_cot = lax.all_gather(cotangent, "tensor", axis=1, tiled=True)

    high, low = two_pieces(merge_weights)
    meta = jnp.concatenate(
        [expert_ids.astype(jnp.float32).reshape(-1), high.reshape(-1), low.reshape(-1)]
    ).astype(jnp.bfloat16)
    meta = jnp.pad(meta[None, :], ((0, PAD - 1), (0, lanes - 3 * listed)))
    table_chunks = split_panels(jnp.transpose(down_table, (1, 0, 2)), count)[:, 0]
    outgoing = jnp.concatenate(
        [table_chunks, jnp.broadcast_to(meta[None], (count, PAD, lanes))], axis=1
    )
    arrived = exchange(outgoing)
    by_slot = arrived[:, :rows]
    meta_all = arrived[:, rows, : 3 * listed].astype(jnp.float32)
    ids_all = meta_all[:, :listed].astype(jnp.int32).reshape(count * seg_count, K)
    high_all = meta_all[:, listed : 2 * listed].reshape(count * seg_count, K)
    low_all = meta_all[:, 2 * listed :].reshape(count * seg_count, K)
    experts = jnp.arange(E, dtype=jnp.int32)
    slots_all = jnp.sum(
        jnp.where(ids_all[:, :, None] == experts, owner_slot[None, None, :], 0), axis=2
    )
    hits = slots_all[:, :, None] == jnp.arange(count, dtype=jnp.int32)
    coef = jnp.concatenate(
        [
            jnp.sum(jnp.where(hits, high_all[:, :, None], 0.0), axis=1),
            jnp.sum(jnp.where(hits, low_all[:, :, None], 0.0), axis=1),
        ],
        axis=0,
    ).astype(jnp.bfloat16)
    halves = jnp.einsum("ms,srl->mrl", coef, by_slot, preferred_element_type=jnp.float32)
    merged_chunks = (halves[: count * seg_count] + halves[count * seg_count :]).astype(jnp.bfloat16)
    merged = join_panels(exchange(merged_chunks.reshape(count, seg_count, rows, lanes)))

    hidden_seg = hidden_act.reshape(seg_count, seg_len, ff_local)
    cot_seg = full_cot.reshape(seg_count, seg_len, width)
    seg_grads = jnp.einsum(
        "stf,std->sfd", hidden_seg, cot_seg, preferred_element_type=jnp.float32
    ).astype(jnp.bfloat16)
    returned = exchange(split_panels(seg_grads, count)).reshape(count * seg_count, rows, lanes)

    partial_rows = jnp.einsum(
        "stf,sfd->std", hidden_seg, merged, preferred_element_type=jnp.float32
    ).reshape(row_count, width)
    layer_out = lax.psum_scatter(
        partial_rows.astype(jnp.bfloat16), "tensor", scatter_dimension=1, tiled=True
    )
    grad_hidden = (
        jnp.einsum("std,sfd->stf", cot_seg, merged, preferred_element_type=jnp.float32)
        .astype(jnp.bfloat16)
        .reshape(row_count, ff_local)
    )

    by_segment = jnp.stack([coef[: count * seg_count], coef[count * seg_count :]], axis=1)
    slot_halves = jnp.einsum(
        "mhs,mrl->hsrl", by_segment, returned, preferred_element_type=jnp.float32
    )
    slot_grads = (slot_halves[0] + slot_halves[1]).astype(jnp.bfloat16)
    own_grad = join_panels(exchange(slot_grads)[:, None])
    expert_grad = jnp.transpose(own_grad, (1, 0, 2)).astype(jnp.float32)
    return (layer_out, grad_hidden, expert_grad)


def solution(mesh):
    placed = (
        P("dp", "tensor"),
        P("dp", "tensor"),
        P("tensor", "dp", None),
        P("dp", None),
        P("dp", None),
        P(),
    )
    return jax.shard_map(
        body,
        mesh=mesh,
        in_specs=placed,
        out_specs=(P("dp", "tensor"), P("dp", "tensor"), P("tensor", "dp", None)),
        check_vma=False,
    )
```

time: 480 us -> 179 us (0.37)
  blocking collectives: 140 us -> 0 us
  waiting for transfers between devices: 176 us -> 105 us
  local copies, waits for them, and re-layouts: 72.6 us -> 16.5 us
  other arithmetic: 36.2 us -> 4.78 us
    all_gather x2 -> x0, blocking collectives: 104 us -> none  [the longest x1 53.9 us: body(): lax.all_gather(merge_weights, 'dp', axis=0, tiled=True)]
    all_to_all x3 -> x4, waiting for transfers between devices: 123 us -> 83.7 us  [exchange(): return lax.all_to_all(blocks, 'dp', split_axis=0, concat_axis=0, tiled=True)]
    all_to_all x1 -> x0, blocking collectives: 35.5 us -> none  [body(): lax.all_to_all(slotted.astype(jnp.bfloat16), 'dp', split_axis=1, concat_a...]
    all_gather x1, waiting for transfers between devices: 53 us -> 20.5 us  [body(): full_cot = lax.all_gather(cotangent, 'tensor', axis=1, tiled=True)]
    select_n x1 -> x0, local copies, waits for them, and re-layouts: 22.3 us -> none  [body(): jnp.take(by_expert, pools_all.T, axis=1).reshape(ff_local, POOL, width)]
    unnamed x20 -> x8, local copies, waits for them, and re-layouts: 17.2 us -> 1.62 us
    gather x2 -> x0, local copies, waits for them, and re-layouts: 13.9 us -> none  [the longest x1 13.3 us: body(): jnp.take(by_expert, pools_all.T, axis=1).reshape(ff_local, POOL, width)]
    unnamed x1 -> x0, other arithmetic: 11.6 us -> none
  transfers between devices with their start and end apart: 5 -> 6, of which waited for: 2 -> 5; matrix products, arithmetic and copies ran while one was open for 11% -> 13% of each run, Pallas kernels for 0% -> 0%
where the time goes in v1:
time: 179 us; the launch traced here: 178 us
  waiting for transfers between devices  105 us (59%)
  starting transfers between devices  31.1 us (17%)
  local copies, waits for them, and re-layouts  16.5 us (9%)
  between operations  14.2 us (8%)
  matrix products  6.5 us (4%)
  other arithmetic  4.78 us (3%)
    all_to_all x4, waiting for transfers between devices, exchange(): return lax.all_to_all(blocks, 'dp', split_axis=0, concat_axis=0, tiled=True)  83.7 us
    all_to_all x4, starting transfers between devices, exchange(): return lax.all_to_all(blocks, 'dp', split_axis=0, concat_axis=0, tiled=True)  30.9 us
    all_gather x1, waiting for transfers between devices, body(): full_cot = lax.all_gather(cotangent, 'tensor', axis=1, tiled=True)  20.5 us
  transfers between devices with their start and end apart: 6, of which 5 were waited for; matrix products, arithmetic and copies ran while one was open for 13% of the time, Pallas kernels for 0%

profile of v1, /device:TPU:1, one launch (start us, length us, event | category | flops | bytes accessed | tf_op | source)
XLA Modules:
  0.0 178.1 jit_solution(396525168196531516)
XLA Ops:
  8.8 1.3 copy.65
  10.4 1.0 pad_maximum_fusion
  11.4 11.8 %all-to-all-start = ((bf16[64,48,128]{2,1,0:T(8,128)(2,1)}), bf16[64,48,128]{2,1,0:T(8,128)(2,1)S(1)}, u32[]{:S(2)}, u32[]{:S(2)}) async-start(bf16[64,48,128]{2,1,0:T(8,128)(2,1)} %pad_maximum_fusion), calls=%async_computation | async-start | bytes 1572864 | tf_op jit(solution)/shard_map/all_to_all | solution.py:19
  23.9 22.0 %all-to-all-done = bf16[64,48,128]{2,1,0:T(8,128)(2,1)S(1)} async-done(((bf16[64,48,128]{2,1,0:T(8,128)(2,1)}), bf16[64,48,128]{2,1,0:T(8,128)(2,1)S(1)}, u32[]{:S(2)}, u32[]{:S(2)}) %all-to-all-start) | async-done | bytes 786464 | tf_op jit(solution)/shard_map/all_to_all | solution.py:19
  46.6 0.9 fusion.4
  48.1 2.1 %copy.51 = bf16[64,2,44,128]{3,1,2,0:T(2,128)(2,1)} copy(bf16[64,2,44,128]{3,1,0,2:T(2,128)(2,1)S(1)} %bitcast.66) | data formatting | bytes 2883584 | tf_op jit(solution)/shard_map/reshape | solution.py:79
  50.2 6.4 %all-to-all-start.1 = ((bf16[64,2,44,128]{3,1,2,0:T(2,128)(2,1)}), bf16[64,2,44,128]{3,1,2,0:T(2,128)(2,1)S(1)}, u32[]{:S(2)}, u32[]{:S(2)}) async-start(bf16[64,2,44,128]{3,1,2,0:T(2,128)(2,1)} %copy.51), calls=%async_computation.1 | async-start | bytes 2883584 | tf_op jit(solution)/shard_map/all_to_all | solution.py:19
  56.6 20.5 %all-gather.2.cloned.1.call-done = bf16[512,2048]{1,0:T(8,128)(2,1)} async-done(((bf16[512,256]{1,0:T(8,128)(2,1)}), bf16[512,2048]{1,0:T(8,128)(2,1)}) %all-gather.2.cloned.1.call-update) | async-done | bytes 2097168 | tf_op jit(solution)/shard_map/all_gather | solution.py:48
  77.1 2.1 %convolution_convert_fusion.1 = bf16[2,176,2048]{2,1,0:T(8,128)(2,1)S(1)} fusion(bf16[2,256,2048]{2,1,0:T(8,128)(2,1)} %bitcast.63, bf16[22,2,8,256]{3,2,1,0:T(8,128)(2,1)S(1)} %bitcast.77), kind=kOutput, calls=%fused_computation.3 | convolution fusion | flops 369819648 | bytes 3719168 | tf_op jit(solution)/shard_map/stf,std->sfd/dot_general | solution.py:83
  80.0 2.6 %copy.57 = bf16[64,2,44,128]{3,1,2,0:T(2,128)(2,1)} copy(bf16[64,2,44,128]{3,0,2,1:T(8,128)(2,1)S(1)} %bitcast.71) | data formatting | bytes 2883584 | tf_op jit(solution)/shard_map/reshape | solution.py:26
  82.6 10.3 %all-to-all-done.1 = bf16[64,2,44,128]{3,1,2,0:T(2,128)(2,1)S(1)} async-done(((bf16[64,2,44,128]{3,1,2,0:T(2,128)(2,1)}), bf16[64,2,44,128]{3,1,2,0:T(2,128)(2,1)S(1)}, u32[]{:S(2)}, u32[]{:S(2)}) %all-to-all-start.1) | async-done | bytes 1441824 | tf_op jit(solution)/shard_map/all_to_all | solution.py:19
  92.9 6.3 %all-to-all-start.2 = ((bf16[64,2,44,128]{3,1,2,0:T(2,128)(2,1)}), bf16[64,2,44,128]{3,1,2,0:T(2,128)(2,1)S(1)}, u32[]{:S(2)}, u32[]{:S(2)}) async-start(bf16[64,2,44,128]{3,1,2,0:T(2,128)(2,1)} %copy.57), calls=%async_computation.3 | async-start | bytes 2883584 | tf_op jit(solution)/shard_map/all_to_all | solution.py:19
  99.4 1.3 copy.78
  100.7 2.5 %reshape.114 = bf16[2,176,2048]{2,1,0:T(8,128)(2,1)S(1)} reshape(bf16[2,4,44,16,128]{4,3,2,1,0:T(8,128)(2,1)} %bitcast.72) | data formatting | bytes 2883584 | tf_op jit(solution)/shard_map/reshape | solution.py:35
  103.2 2.1 %convolution_convert_fusion = bf16[2,2048,256]{1,2,0:T(8,128)(2,1)} fusion(bf16[2,176,2048]{2,1,0:T(8,128)(2,1)S(1)} %reshape.114, bf16[22,2,8,256]{3,2,1,0:T(8,128)(2,1)S(1)} %bitcast.78), kind=kOutput, calls=%fused_computation | convolution fusion | flops 370147328 | bytes 3719168 | tf_op jit(solution)/shard_map/stf,sfd->std/dot_general | solution.py:88
  105.3 30.3 %all-to-all-done.2 = bf16[64,2,44,128]{3,1,2,0:T(2,128)(2,1)S(1)} async-done(((bf16[64,2,44,128]{3,1,2,0:T(2,128)(2,1)}), bf16[64,2,44,128]{3,1,2,0:T(2,128)(2,1)S(1)}, u32[]{:S(2)}, u32[]{:S(2)}) %all-to-all-start.2) | async-done | bytes 1441824 | tf_op jit(solution)/shard_map/all_to_all | solution.py:19
  135.6 1.5 copy.58
  137.9 1.4 copy.59
  139.3 6.5 %all-to-all-start.3 = ((bf16[64,44,128]{2,1,0:T(8,128)(2,1)}), bf16[64,44,128]{2,1,0:T(8,128)(2,1)}, u32[]{:S(2)}, u32[]{:S(2)}) async-start(bf16[64,44,128]{2,1,0:T(8,128)(2,1)} %copy.59), calls=%async_computation.4 | async-start | bytes 1572864 | tf_op jit(solution)/shard_map/all_to_all | solution.py:19
  145.8 0.8 fusion.2
  146.6 0.7 copy.64
  147.3 21.1 %all-to-all-done.3 = bf16[64,44,128]{2,1,0:T(8,128)(2,1)} async-done(((bf16[64,44,128]{2,1,0:T(8,128)(2,1)}), bf16[64,44,128]{2,1,0:T(8,128)(2,1)}, u32[]{:S(2)}, u32[]{:S(2)}) %all-to-all-start.3) | async-done | bytes 720928 | tf_op jit(solution)/shard_map/all_to_all | solution.py:19
  168.5 1.3 convert_bitcast_fusion
  169.7 1.5 copy.60
  (34 shorter events, 5.7 us)
Async XLA Ops:
  11.4 35.1 %copy-start.2 = (s32[32]{0:T(128)S(1)}, s32[32]{0:T(128)}, u32[]{:S(2)}) copy-start(s32[32]{0:T(128)} %param.11) | copy-start | bytes 388
  11.4 34.5 %all-to-all-start = ((bf16[64,48,128]{2,1,0:T(8,128)(2,1)}), bf16[64,48,128]{2,1,0:T(8,128)(2,1)S(1)}, u32[]{:S(2)}, u32[]{:S(2)}) async-start(bf16[64,48,128]{2,1,0:T(8,128)(2,1)} %pad_maximum_fusion), calls=%async_computation | async-start | bytes 1572864 | tf_op jit(solution)/shard_map/all_to_all | solution.py:19
  23.1 54.0 %all-gather.2.cloned.1.call-start = ((), (), s32[]{:S(2)}) async-start(), calls=%async_computation.6 | async-start | bytes 2359296 | tf_op jit(solution)/shard_map/all_gather | solution.py:48
  50.2 26.9 %copy-start.1 = (bf16[512,176]{0,1:T(8,128)(2,1)S(1)}, bf16[512,176]{0,1:T(8,128)(2,1)}, u32[]{:S(2)}) copy-start(bf16[512,176]{0,1:T(8,128)(2,1)} %param.6) | copy-start | bytes 540676
  50.2 42.7 %all-to-all-start.1 = ((bf16[64,2,44,128]{3,1,2,0:T(2,128)(2,1)}), bf16[64,2,44,128]{3,1,2,0:T(2,128)(2,1)S(1)}, u32[]{:S(2)}, u32[]{:S(2)}) async-start(bf16[64,2,44,128]{3,1,2,0:T(2,128)(2,1)} %copy.51), calls=%async_computation.1 | async-start | bytes 2883584 | tf_op jit(solution)/shard_map/all_to_all | solution.py:19
  92.9 42.7 %all-to-all-start.2 = ((bf16[64,2,44,128]{3,1,2,0:T(2,128)(2,1)}), bf16[64,2,44,128]{3,1,2,0:T(2,128)(2,1)S(1)}, u32[]{:S(2)}, u32[]{:S(2)}) async-start(bf16[64,2,44,128]{3,1,2,0:T(2,128)(2,1)} %copy.57), calls=%async_computation.3 | async-start | bytes 2883584 | tf_op jit(solution)/shard_map/all_to_all | solution.py:19
  99.2 72.1 %reduce-scatter.2.cloned.1.call-start = ((), (), s32[]{:S(2)}) async-start(), calls=%async_computation.5 | async-start | bytes 2359296 | tf_op jit(solution)/shard_map/reduce_scatter | solution.py:91
  137.9 7.8 %copy-start = (bf16[512,2048]{1,0:T(8,128)(2,1)S(1)}, bf16[512,2048]{1,0:T(8,128)(2,1)}, u32[]{:S(2)}) copy-start(bf16[512,2048]{1,0:T(8,128)(2,1)} %all-gather.2.cloned.1.call-done) | copy-start | bytes 6291460
  139.3 29.2 %all-to-all-start.3 = ((bf16[64,44,128]{2,1,0:T(8,128)(2,1)}), bf16[64,44,128]{2,1,0:T(8,128)(2,1)}, u32[]{:S(2)}, u32[]{:S(2)}) async-start(bf16[64,44,128]{2,1,0:T(8,128)(2,1)} %copy.59), calls=%async_computation.4 | async-start | bytes 1572864 | tf_op jit(solution)/shard_map/all_to_all | solution.py:19
Sparse Core Ops, SparseCore 0:
  26.0 51.0 all-gather.1
  105.4 45.6 reduce-scatter.1
